TPU v7x, 32 devices: a whole 2x2x4 slice. The times are simulated.
32 devices in a mesh: col: 4 (over y, core), fac: 8 (over z, x).
Axes of the slice: x: 2, y: 2, z: 4, core: 2. Of those that a mesh axis runs over, the one named last changes fastest.
Arguments:
- facets: bfloat16 [2, 4096, 4096], P(None, 'col', 'fac'), may hold values from -6 to 6
- row_taper: float32 [4096], P('col'), may hold values from 0.5 to 1.5
- column_taper: float32 [4096], replicated, may hold values from 0.5 to 1.5
- column_place: int32 [1], replicated, may hold values from 0 to 511
- row_offset: int32 [4], replicated, may hold values from 0 to 4095
- column_offset: int32 [8], replicated, may hold values from 0 to 4095
- slot_subgrid: int32 [4, 8], replicated, may hold values from 0 to 7, each once within a row
Outputs:
- subgrids: float32 [4, 8, 2, 512, 128], P('col', 'fac')
All inputs are finite; a program needn't handle non-finite values.
Results may differ from a plain program's by a relative error of at most 0.0052.
Values may be sent and summed in bfloat16 or wider, within the bound.
A program may use at most 64 MiB of HBM per device.

v0:
```python
import functools
import math

import jax
import jax.numpy as jnp
from jax import lax
from jax.experimental import pallas as pl
from jax.experimental.pallas import tpu as pltpu
from jax.sharding import PartitionSpec as P

FACET = 4096
STRIP = 128
SUBGRID = 512
FINE = 16
CHUNKS = 4
LAG = 2
CHUNK = STRIP // CHUNKS
MESH = pl.DeviceIdType.MESH


def unit_phase(phases):
    quarter = FACET // 4
    shifted = phases + quarter // 2
    angle = ((shifted & (quarter - 1)) - quarter // 2).astype(jnp.float32) * (2.0 * math.pi / FACET)
    turn = lax.shift_right_logical(shifted & (FACET - 1), quarter.bit_length() - 1)
    sq = angle * angle
    cosine = 1.0 + sq * (-1 / 2 + sq * (1 / 24 + sq * (-1 / 720 + sq * (1 / 40320))))
    sine = angle * (1.0 + sq * (-1 / 6 + sq * (1 / 120 + sq * (-1 / 5040 + sq * (1 / 362880)))))
    odd = (turn & 1) == 1
    first = jnp.where(odd, sine, cosine)
    second = jnp.where(odd, cosine, sine)
    real = jnp.where(((turn + 1) & 2) == 2, -first, first)
    imag = jnp.where((turn & 2) == 2, second, -second)
    return real, imag


def iota(shape, dim):
    return lax.broadcasted_iota(jnp.int32, shape, dim)


def kernel(
    cols, facs,
    row_offset_in, column_offset_in, slot_subgrid_in, row_taper_in, column_taper_in, facets,
    out,
    row_offset, column_offset, slot_subgrid, row_taper, column_gain, held, coarse_r, coarse_i, fine_r, fine_i, steep_r, steep_i, encode, decode_r, decode_i,
    pair_out, pair_in, far_part, far_out, far_in, own_part, strip, strip_in,
    half, mine, slots_out, slots_in,
    small_sem, held_sem, pair_send, pair_recv, far_send, far_recv, strip_send, strip_recv, slot_send, slot_recv,
):
    col = lax.axis_index("col")
    fac = lax.axis_index("fac")
    col_hi, core = col // 2, col % 2
    fac_hi, fac_lo = fac // 2, fac % 2
    highs, zs = cols // 2, facs // 2
    rows, width = facets.shape[1], facets.shape[2]

    pair_id = (col_hi * 2 + 1 - core, fac)
    far_ids = [((col_hi + d) % highs * 2 + core, fac) for d in range(1, highs)]
    strip_id = (col, fac_hi * 2 + 1 - fac_lo)
    slot_ids = [(col, (fac_hi + d) % zs * 2 + fac_lo) for d in range(1, zs)]
    peers = [pair_id, *far_ids, strip_id, *slot_ids]
    own_columns = pl.ds(pl.multiple_of(fac * width, width), width)
    small = [
        pltpu.make_async_copy(source, target, small_sem.at[n])
        for n, (source, target) in enumerate((
            (row_offset_in, row_offset), (column_offset_in, column_offset), (slot_subgrid_in, slot_subgrid),
            (row_taper_in, row_taper),
            (column_taper_in.at[:, own_columns], column_gain)))]
    loads = [pltpu.make_async_copy(facets.at[p], held.at[p], held_sem.at[p]) for p in range(2)]
    for load in (*small, *loads):
        load.start()
    barrier = pltpu.get_barrier_semaphore()
    for peer in peers:
        pl.semaphore_signal(barrier, inc=1, device_id=peer, device_id_type=MESH)

    steps = STRIP // FINE
    position = col * rows + iota((1, rows), 1)
    fine_r[...], fine_i[...] = unit_phase(iota((FINE, rows), 0) * position)
    for load in small:
        load.wait()
    gain = row_taper[...] * (1.0 / math.sqrt(FACET))

    def encode_group(index, group):
        first = (row_offset[group] + FINE * iota((steps, rows), 0)) & (FACET - 1)
        real, imag = unit_phase(first * position)
        coarse_r[...] = real * gain
        coarse_i[...] = imag * gain

        def row(i, carry):
            ar, ai = coarse_r[pl.ds(i, 1), :], coarse_i[pl.ds(i, 1), :]
            br, bi = fine_r[...], fine_i[...]
            at = pl.multiple_of(i * FINE, FINE)
            encode[index, pl.ds(at, FINE), :] = (ar * br - ai * bi).astype(jnp.bfloat16)
            encode[index, pl.ds(at + STRIP, FINE), :] = (ar * bi + ai * br).astype(jnp.bfloat16)
            return carry

        lax.fori_loop(0, steps, row, 0)

    def product(index):
        table = encode[index]
        by_real = jnp.dot(table, held[0], preferred_element_type=jnp.float32)
        by_imag = jnp.dot(table, held[1], preferred_element_type=jnp.float32)
        return by_real[:STRIP] - by_imag[STRIP:], by_imag[:STRIP] + by_real[STRIP:]

    def chunked(target, real, imag):
        for j in range(CHUNKS):
            span = slice(j * CHUNK, (j + 1) * CHUNK)
            target[j, :CHUNK] = real[span].astype(target.dtype)
            target[j, CHUNK:] = imag[span].astype(target.dtype)

    def pair_copy(d, j):
        return pltpu.make_async_remote_copy(
            src_ref=pair_out.at[d, j], dst_ref=pair_in.at[d, j], send_sem=pair_send.at[d, j],
            recv_sem=pair_recv.at[d, j], device_id=pair_id, device_id_type=MESH)

    def far_copy(d, j):
        return pltpu.make_async_remote_copy(
            src_ref=far_out.at[d - 1, j], dst_ref=far_in.at[d - 1, j], send_sem=far_send.at[d - 1, j],
            recv_sem=far_recv.at[d - 1, j], device_id=far_ids[d - 1], device_id_type=MESH)

    def strip_copy(j):
        return pltpu.make_async_remote_copy(
            src_ref=strip.at[j], dst_ref=strip_in.at[j], send_sem=strip_send.at[j],
            recv_sem=strip_recv.at[j], device_id=strip_id, device_id_type=MESH)

    def slot_copy(d, j):
        return pltpu.make_async_remote_copy(
            src_ref=slots_out.at[d - 1, j], dst_ref=slots_in.at[d - 1, j], send_sem=slot_send.at[d - 1, j],
            recv_sem=slot_recv.at[d - 1, j], device_id=slot_ids[d - 1], device_id_type=MESH)

    def groups(d):
        high = (col_hi + d) % highs * 2
        encode_group(2 * d, high + 1 - core)
        encode_group(2 * d + 1, high + core)

    for d in range(1, highs):
        groups(d)
    for load in loads:
        load.wait()
    for d in range(1, highs):
        chunked(pair_out.at[d], *product(2 * d))
        chunked(far_part.at[d - 1], *product(2 * d + 1))
    pl.semaphore_wait(barrier, len(peers))
    for d in range(1, highs):
        for j in range(CHUNKS):
            pair_copy(d, j).start()
    groups(0)
    chunked(pair_out.at[0], *product(0))
    for j in range(CHUNKS):
        pair_copy(0, j).start()
    for d in range(1, highs):
        for j in range(CHUNKS):
            pair_copy(d, j).wait_recv()
            far_out[d - 1, j] = (far_part[d - 1, j] + pair_in[d, j].astype(jnp.float32)).astype(jnp.bfloat16)
            far_copy(d, j).start()
    chunked(own_part, *product(1))

    lanes = zs * STRIP
    coarse_n = width // FINE
    starts = []
    for d in range(zs):
        start = column_offset[slot_subgrid[col, (fac_hi + d) % zs * 2 + fac_lo]]
        starts.append((start + iota((1, STRIP), 1)) & (FACET - 1))
    frequency = jnp.concatenate(starts, axis=1)
    fine_real, fine_imag = unit_phase(iota((FINE, lanes), 0) * frequency)
    fine_real, fine_imag = fine_real * (1.0 / math.sqrt(FACET)), fine_imag * (1.0 / math.sqrt(FACET))
    for part, block in enumerate((fac, fac_hi * 2 + 1 - fac_lo)):
        base = part * width
        steep_r[...], steep_i[...] = unit_phase((block * width + FINE * iota((coarse_n, lanes), 0)) * frequency)

        def row(i, carry, base=base):
            ar, ai = steep_r[pl.ds(i, 1), :], steep_i[pl.ds(i, 1), :]
            at = pl.multiple_of(base + i * FINE, FINE)
            decode_r[pl.ds(at, FINE), :] = (ar * fine_real - ai * fine_imag).astype(jnp.bfloat16)
            decode_i[pl.ds(at, FINE), :] = (ar * fine_imag + ai * fine_real).astype(jnp.bfloat16)
            return carry

        lax.fori_loop(0, coarse_n, row, 0)

    def decoded(block, part):
        span = slice(part * width, (part + 1) * width)
        by_real = jnp.dot(block, decode_r[span], preferred_element_type=jnp.float32)
        by_imag = jnp.dot(block, decode_i[span], preferred_element_type=jnp.float32)
        return jnp.concatenate(
            [by_real[:CHUNK] - by_imag[CHUNK:], by_imag[:CHUNK] + by_real[CHUNK:]], axis=0)

    def finish(j):
        strip_copy(j).wait_recv()
        total = half[j] + decoded(strip_in[j], 1)
        mine[j] = total[:, :STRIP]
        for d in range(1, zs):
            slots_out[d - 1, j] = total[:, d * STRIP:(d + 1) * STRIP].astype(jnp.bfloat16)
            slot_copy(d, j).start()

    for j in range(CHUNKS):
        pair_copy(0, j).wait_recv()
        total = own_part[j] + pair_in[0, j].astype(jnp.float32)
        for d in range(1, highs):
            far_copy(d, j).wait_recv()
            total = total + far_in[d - 1, j].astype(jnp.float32)
        strip[j] = (total * column_gain[...]).astype(jnp.bfloat16)
        strip_copy(j).start()
        half[j] = decoded(strip[j], 0)
        if j >= LAG:
            finish(j - LAG)
    for j in range(CHUNKS - LAG, CHUNKS):
        finish(j)

    sums = []
    for j in range(CHUNKS):
        total = mine[j]
        for d in range(1, zs):
            slot_copy(d, j).wait_recv()
            total = total + slots_in[d - 1, j].astype(jnp.float32)
        sums.append(total)
    for part in range(2):
        value = jnp.concatenate([s[part * CHUNK:(part + 1) * CHUNK] for s in sums], axis=0)
        out[part] = value.T

    for j in range(CHUNKS):
        for d in range(highs):
            pair_copy(d, j).wait_send()
        for d in range(1, highs):
            far_copy(d, j).wait_send()
        strip_copy(j).wait_send()
        for d in range(1, zs):
            slot_copy(d, j).wait_send()


def place_kernel(place, part, out):
    blank = jnp.zeros((SUBGRID - STRIP, STRIP), jnp.float32)
    for n in range(2):
        out[n] = pltpu.roll(jnp.concatenate([part[n], blank], axis=0), place[0], 0)


def solution(mesh):
    cols, facs = mesh.shape["col"], mesh.shape["fac"]
    highs, zs = cols // 2, facs // 2

    def on_device(facets, row_taper, column_taper, column_place, row_offset, column_offset, slot_subgrid):
        rows, width = facets.shape[1], facets.shape[2]
        bf16, f32 = jnp.bfloat16, jnp.float32
        lanes = zs * STRIP
        part = (CHUNKS, 2 * CHUNK, width)
        slot = (CHUNKS, 2 * CHUNK, STRIP)
        far = max(highs - 1, 1)
        sem = pltpu.SemaphoreType.DMA
        grid = pl.pallas_call(
            functools.partial(kernel, cols, facs),
            out_shape=jax.ShapeDtypeStruct((2, STRIP, STRIP), f32),
            in_specs=[pl.BlockSpec(memory_space=pltpu.HBM)] * 6,
            out_specs=pl.BlockSpec(memory_space=pltpu.VMEM),
            scratch_shapes=[
                pltpu.SMEM(row_offset.shape, jnp.int32), pltpu.SMEM(column_offset.shape, jnp.int32),
                pltpu.SMEM(slot_subgrid.shape, jnp.int32),
                pltpu.VMEM((1, rows), f32), pltpu.VMEM((1, width), f32),
                pltpu.VMEM((2, rows, width), bf16),
                pltpu.VMEM((STRIP // FINE, rows), f32), pltpu.VMEM((STRIP // FINE, rows), f32),
                pltpu.VMEM((FINE, rows), f32), pltpu.VMEM((FINE, rows), f32),
                pltpu.VMEM((width // FINE, lanes), f32), pltpu.VMEM((width // FINE, lanes), f32),
                pltpu.VMEM((cols, 2 * STRIP, rows), bf16),
                pltpu.VMEM((2 * width, lanes), bf16), pltpu.VMEM((2 * width, lanes), bf16),
                pltpu.VMEM((highs, *part), bf16), pltpu.VMEM((highs, *part), bf16),
                pltpu.VMEM((far, *part), f32),
                pltpu.VMEM((far, *part), bf16), pltpu.VMEM((far, *part), bf16),
                pltpu.VMEM(part, f32),
                pltpu.VMEM(part, bf16), pltpu.VMEM(part, bf16),
                pltpu.VMEM((CHUNKS, 2 * CHUNK, lanes), f32),
                pltpu.VMEM(slot, f32),
                pltpu.VMEM((zs - 1, *slot), bf16), pltpu.VMEM((zs - 1, *slot), bf16),
                sem((5,)), sem((2,)),
                sem((highs, CHUNKS)), sem((highs, CHUNKS)),
                sem((far, CHUNKS)), sem((far, CHUNKS)),
                sem((CHUNKS,)), sem((CHUNKS,)),
                sem((zs - 1, CHUNKS)), sem((zs - 1, CHUNKS)),
            ],
            compiler_params=pltpu.CompilerParams(
                collective_id=0, has_side_effects=True, vmem_limit_bytes=67_043_328),
        )(row_offset, column_offset, slot_subgrid,
          row_taper.reshape(1, -1), column_taper.reshape(1, -1), facets)
        grid = pl.pallas_call(
            place_kernel,
            out_shape=jax.ShapeDtypeStruct((2, SUBGRID, STRIP), f32),
            in_specs=[pl.BlockSpec(memory_space=pltpu.SMEM), pl.BlockSpec(memory_space=pltpu.VMEM)],
            out_specs=pl.BlockSpec(memory_space=pltpu.VMEM),
        )(column_place, grid)
        return grid.reshape(1, 1, 2, SUBGRID, STRIP)

    in_specs = (P(None, "col", "fac"), P("col"), P(), P(), P(), P(), P())
    out_specs = P("col", "fac", None, None, None)
    return jax.shard_map(on_device, mesh=mesh, in_specs=in_specs, out_specs=out_specs, check_vma=False)
```

profile of v0, /device:TPU:0, one launch (start us, length us, event | category | flops | bytes accessed | tf_op | source)
XLA Modules:
  0.0 27.1 jit_solution(13452593477009906048)
XLA Ops:
  0.7 24.7 %shard_map.73.part = f32[2,128,128]{2,1,0:T(8,128)} custom-call(s32[4]{0:T(128)} %row_offset_in.1, s32[8]{0:T(128)} %column_offset_in.1, s32[4,8]{1,0:T(4,128)} %slot_subgrid_in.1, f32[1,1024]{1,0:T(1,128)} %bitcast.4, f32[1,4096]{1,0:T(1,128)} %bitcast.3, bf16[2,1024,512]{2,1,0:T(8,128)(2,1)} %facets.1), custom_call_target="tpu_custom_call" | custom-call | tf_op jit(solution)/shard_map/pallas_call | solution.py:248
  25.3 1.8 %shard_map.74 = f32[2,512,128]{2,1,0:T(8,128)} custom-call(s32[1]{0:T(128)S(6)} %copy.8.place, f32[2,128,128]{2,1,0:T(8,128)} %shard_map.73.part), custom_call_target="tpu_custom_call" | custom-call | tf_op jit(solution)/shard_map/pallas_call | solution.py:281
where the time goes:
time: 27.3 us; the launch traced here: 27.1 us
  Pallas kernels  26.5 us (97%)
  between operations  0.66 us (2%)
    pallas_call x1, Pallas kernels, on_device(): pl.pallas_call(functools.partial(kernel, cols, facs), out_shape=jax.Shape...  24.7 us
    pallas_call x1, Pallas kernels, on_device(): pl.pallas_call(place_kernel, out_shape=jax.ShapeDtypeStruct((2, SUBGRID,...  1.78 us

commit v1 on v0

--- a/solution.py
+++ b/solution.py
@@ -12,9 +12,10 @@
 STRIP = 128
 SUBGRID = 512
 FINE = 16
-CHUNKS = 4
-LAG = 2
-CHUNK = STRIP // CHUNKS
+SIZES = (32, 32, 32, 32)
+CHUNKS = len(SIZES)
+PIECES = 2
+HOP_ROWS = 60
 MESH = pl.DeviceIdType.MESH
 
 
@@ -32,6 +33,20 @@
     real = jnp.where(((turn + 1) & 2) == 2, -first, first)
     imag = jnp.where((turn & 2) == 2, second, -second)
     return real, imag
+
+
+def span(j):
+    start = 2 * sum(SIZES[:j])
+    return slice(start, start + 2 * SIZES[j])
+
+
+def order():
+    far_done, free, events = 0, 0, []
+    for j, size in enumerate(SIZES):
+        far_done += size
+        free = max(free, far_done) + size
+        events += [(far_done, 0, j), (free + HOP_ROWS, 1, j)]
+    return [event[1:] for event in sorted(events)]
 
 
 def iota(shape, dim):
@@ -66,7 +81,9 @@
             (row_offset_in, row_offset), (column_offset_in, column_offset), (slot_subgrid_in, slot_subgrid),
             (row_taper_in, row_taper),
             (column_taper_in.at[:, own_columns], column_gain)))]
-    loads = [pltpu.make_async_copy(facets.at[p], held.at[p], held_sem.at[p]) for p in range(2)]
+    depth = rows // PIECES
+    pieces = [slice(n * depth, (n + 1) * depth) for n in range(PIECES)]
+    loads = [pltpu.make_async_copy(facets.at[:, piece], held.at[:, piece], held_sem.at[n]) for n, piece in enumerate(pieces)]
     for load in (*small, *loads):
         load.start()
     barrier = pltpu.get_barrier_semaphore()
@@ -96,63 +113,73 @@
 
         lax.fori_loop(0, steps, row, 0)
 
+    def combined(by_real, by_imag):
+        return by_real[:STRIP] - by_imag[STRIP:], by_imag[:STRIP] + by_real[STRIP:]
+
     def product(index):
         table = encode[index]
-        by_real = jnp.dot(table, held[0], preferred_element_type=jnp.float32)
-        by_imag = jnp.dot(table, held[1], preferred_element_type=jnp.float32)
-        return by_real[:STRIP] - by_imag[STRIP:], by_imag[:STRIP] + by_real[STRIP:]
+        return combined(*[jnp.dot(table, held[p], preferred_element_type=jnp.float32) for p in range(2)])
+
+    def first_product(index):
+        sums = [None, None]
+        for load, piece in zip(loads, pieces):
+            load.wait()
+            table = encode[index, :, piece]
+            for p in range(2):
+                term = jnp.dot(table, held[p, piece], preferred_element_type=jnp.float32)
+                sums[p] = term if sums[p] is None else sums[p] + term
+        return combined(*sums)
 
     def chunked(target, real, imag):
-        for j in range(CHUNKS):
-            span = slice(j * CHUNK, (j + 1) * CHUNK)
-            target[j, :CHUNK] = real[span].astype(target.dtype)
-            target[j, CHUNK:] = imag[span].astype(target.dtype)
+        for j, size in enumerate(SIZES):
+            start = span(j).start
+            target[start:start + size] = real[start // 2:start // 2 + size].astype(target.dtype)
+            target[start + size:start + 2 * size] = imag[start // 2:start // 2 + size].astype(target.dtype)
 
     def pair_copy(d, j):
         return pltpu.make_async_remote_copy(
-            src_ref=pair_out.at[d, j], dst_ref=pair_in.at[d, j], send_sem=pair_send.at[d, j],
+            src_ref=pair_out.at[d, span(j)], dst_ref=pair_in.at[d, span(j)], send_sem=pair_send.at[d, j],
             recv_sem=pair_recv.at[d, j], device_id=pair_id, device_id_type=MESH)
 
     def far_copy(d, j):
         return pltpu.make_async_remote_copy(
-            src_ref=far_out.at[d - 1, j], dst_ref=far_in.at[d - 1, j], send_sem=far_send.at[d - 1, j],
+            src_ref=far_out.at[d - 1, span(j)], dst_ref=far_in.at[d - 1, span(j)], send_sem=far_send.at[d - 1, j],
             recv_sem=far_recv.at[d - 1, j], device_id=far_ids[d - 1], device_id_type=MESH)
 
     def strip_copy(j):
         return pltpu.make_async_remote_copy(
-            src_ref=strip.at[j], dst_ref=strip_in.at[j], send_sem=strip_send.at[j],
+            src_ref=strip.at[span(j)], dst_ref=strip_in.at[span(j)], send_sem=strip_send.at[j],
             recv_sem=strip_recv.at[j], device_id=strip_id, device_id_type=MESH)
 
     def slot_copy(d, j):
         return pltpu.make_async_remote_copy(
-            src_ref=slots_out.at[d - 1, j], dst_ref=slots_in.at[d - 1, j], send_sem=slot_send.at[d - 1, j],
+            src_ref=slots_out.at[d - 1, span(j)], dst_ref=slots_in.at[d - 1, span(j)], send_sem=slot_send.at[d - 1, j],
             recv_sem=slot_recv.at[d - 1, j], device_id=slot_ids[d - 1], device_id_type=MESH)
 
-    def groups(d):
-        high = (col_hi + d) % highs * 2
-        encode_group(2 * d, high + 1 - core)
-        encode_group(2 * d + 1, high + core)
+    def group(d, own):
+        encode_group(2 * d + own, (col_hi + d) % highs * 2 + (core if own else 1 - core))
 
     for d in range(1, highs):
-        groups(d)
-    for load in loads:
-        load.wait()
+        group(d, 0)
+        group(d, 1)
     for d in range(1, highs):
-        chunked(pair_out.at[d], *product(2 * d))
+        chunked(pair_out.at[d], *(first_product(2 * d) if d == 1 else product(2 * d)))
+        if d == 1:
+            pl.semaphore_wait(barrier, len(peers))
+        for j in range(CHUNKS):
+            pair_copy(d, j).start()
         chunked(far_part.at[d - 1], *product(2 * d + 1))
-    pl.semaphore_wait(barrier, len(peers))
     for d in range(1, highs):
         for j in range(CHUNKS):
-            pair_copy(d, j).start()
-    groups(0)
+            pair_copy(d, j).wait_recv()
+            far_out[d - 1, span(j)] = (
+                far_part[d - 1, span(j)] + pair_in[d, span(j)].astype(jnp.float32)).astype(jnp.bfloat16)
+            far_copy(d, j).start()
+    group(0, 0)
     chunked(pair_out.at[0], *product(0))
     for j in range(CHUNKS):
         pair_copy(0, j).start()
-    for d in range(1, highs):
-        for j in range(CHUNKS):
-            pair_copy(d, j).wait_recv()
-            far_out[d - 1, j] = (far_part[d - 1, j] + pair_in[d, j].astype(jnp.float32)).astype(jnp.bfloat16)
-            far_copy(d, j).start()
+    group(0, 1)
     chunked(own_part, *product(1))
 
     lanes = zs * STRIP
@@ -178,43 +205,42 @@
         lax.fori_loop(0, coarse_n, row, 0)
 
     def decoded(block, part):
-        span = slice(part * width, (part + 1) * width)
-        by_real = jnp.dot(block, decode_r[span], preferred_element_type=jnp.float32)
-        by_imag = jnp.dot(block, decode_i[span], preferred_element_type=jnp.float32)
-        return jnp.concatenate(
-            [by_real[:CHUNK] - by_imag[CHUNK:], by_imag[:CHUNK] + by_real[CHUNK:]], axis=0)
+        at = slice(part * width, (part + 1) * width)
+        size = block.shape[0] // 2
+        by_real = jnp.dot(block, decode_r[at], preferred_element_type=jnp.float32)
+        by_imag = jnp.dot(block, decode_i[at], preferred_element_type=jnp.float32)
+        return jnp.concatenate([by_real[:size] - by_imag[size:], by_imag[:size] + by_real[size:]], axis=0)
+
+    def begin(j):
+        pair_copy(0, j).wait_recv()
+        total = own_part[span(j)] + pair_in[0, span(j)].astype(jnp.float32)
+        for d in range(1, highs):
+            far_copy(d, j).wait_recv()
+            total = total + far_in[d - 1, span(j)].astype(jnp.float32)
+        strip[span(j)] = (total * column_gain[...]).astype(jnp.bfloat16)
+        strip_copy(j).start()
+        half[span(j)] = decoded(strip[span(j)], 0)
 
     def finish(j):
         strip_copy(j).wait_recv()
-        total = half[j] + decoded(strip_in[j], 1)
-        mine[j] = total[:, :STRIP]
+        total = half[span(j)] + decoded(strip_in[span(j)], 1)
+        mine[span(j)] = total[:, :STRIP]
         for d in range(1, zs):
-            slots_out[d - 1, j] = total[:, d * STRIP:(d + 1) * STRIP].astype(jnp.bfloat16)
+            slots_out[d - 1, span(j)] = total[:, d * STRIP:(d + 1) * STRIP].astype(jnp.bfloat16)
             slot_copy(d, j).start()
 
-    for j in range(CHUNKS):
-        pair_copy(0, j).wait_recv()
-        total = own_part[j] + pair_in[0, j].astype(jnp.float32)
-        for d in range(1, highs):
-            far_copy(d, j).wait_recv()
-            total = total + far_in[d - 1, j].astype(jnp.float32)
-        strip[j] = (total * column_gain[...]).astype(jnp.bfloat16)
-        strip_copy(j).start()
-        half[j] = decoded(strip[j], 0)
-        if j >= LAG:
-            finish(j - LAG)
-    for j in range(CHUNKS - LAG, CHUNKS):
-        finish(j)
+    for stage, j in order():
+        (begin, finish)[stage](j)
 
     sums = []
     for j in range(CHUNKS):
-        total = mine[j]
+        total = mine[span(j)]
         for d in range(1, zs):
             slot_copy(d, j).wait_recv()
-            total = total + slots_in[d - 1, j].astype(jnp.float32)
+            total = total + slots_in[d - 1, span(j)].astype(jnp.float32)
         sums.append(total)
     for part in range(2):
-        value = jnp.concatenate([s[part * CHUNK:(part + 1) * CHUNK] for s in sums], axis=0)
+        value = jnp.concatenate([s[part * size:(part + 1) * size] for s, size in zip(sums, SIZES)], axis=0)
         out[part] = value.T
 
     for j in range(CHUNKS):
@@ -227,10 +253,19 @@
             slot_copy(d, j).wait_send()
 
 
-def place_kernel(place, part, out):
-    blank = jnp.zeros((SUBGRID - STRIP, STRIP), jnp.float32)
+def place_kernel(place, part, out, grid, sem):
+    shift = lax.rem(place[0], 8)
+    first = pl.multiple_of(place[0] - shift, 8)
+    band = STRIP + 8
+    copies = [pltpu.make_async_copy(grid.at[n, pl.ds(0, SUBGRID)], out.at[n], sem.at[n]) for n in range(2)]
     for n in range(2):
-        out[n] = pltpu.roll(jnp.concatenate([part[n], blank], axis=0), place[0], 0)
+        grid[n] = jnp.zeros(grid.shape[1:], jnp.float32)
+        grid[n, pl.ds(first, band)] = pltpu.roll(
+            jnp.concatenate([part[n], jnp.zeros((8, STRIP), jnp.float32)], axis=0), shift, 0)
+        grid[n, :band] += grid[n, SUBGRID:]
+        copies[n].start()
+    for copy in copies:
+        copy.wait()
 
 
 def solution(mesh):
@@ -241,8 +276,8 @@
         rows, width = facets.shape[1], facets.shape[2]
         bf16, f32 = jnp.bfloat16, jnp.float32
         lanes = zs * STRIP
-        part = (CHUNKS, 2 * CHUNK, width)
-        slot = (CHUNKS, 2 * CHUNK, STRIP)
+        part = (2 * STRIP, width)
+        slot = (2 * STRIP, STRIP)
         far = max(highs - 1, 1)
         sem = pltpu.SemaphoreType.DMA
         grid = pl.pallas_call(
@@ -265,24 +300,26 @@
                 pltpu.VMEM((far, *part), bf16), pltpu.VMEM((far, *part), bf16),
                 pltpu.VMEM(part, f32),
                 pltpu.VMEM(part, bf16), pltpu.VMEM(part, bf16),
-                pltpu.VMEM((CHUNKS, 2 * CHUNK, lanes), f32),
+                pltpu.VMEM((2 * STRIP, lanes), f32),
                 pltpu.VMEM(slot, f32),
                 pltpu.VMEM((zs - 1, *slot), bf16), pltpu.VMEM((zs - 1, *slot), bf16),
-                sem((5,)), sem((2,)),
+                sem((5,)), sem((PIECES,)),
                 sem((highs, CHUNKS)), sem((highs, CHUNKS)),
                 sem((far, CHUNKS)), sem((far, CHUNKS)),
                 sem((CHUNKS,)), sem((CHUNKS,)),
                 sem((zs - 1, CHUNKS)), sem((zs - 1, CHUNKS)),
             ],
             compiler_params=pltpu.CompilerParams(
-                collective_id=0, has_side_effects=True, vmem_limit_bytes=67_043_328),
-        )(row_offset, column_offset, slot_subgrid,
-          row_taper.reshape(1, -1), column_taper.reshape(1, -1), facets)
+                collective_id=0, has_side_effects=True, vmem_limit_bytes=32 * 1024 * 1024),
+        )(*[pltpu.with_memory_space_constraint(value, pltpu.HBM) for value in (
+            row_offset, column_offset, slot_subgrid, row_taper.reshape(1, -1), column_taper.reshape(1, -1), facets)])
         grid = pl.pallas_call(
             place_kernel,
             out_shape=jax.ShapeDtypeStruct((2, SUBGRID, STRIP), f32),
             in_specs=[pl.BlockSpec(memory_space=pltpu.SMEM), pl.BlockSpec(memory_space=pltpu.VMEM)],
-            out_specs=pl.BlockSpec(memory_space=pltpu.VMEM),
+            out_specs=pl.BlockSpec(memory_space=pltpu.HBM),
+            scratch_shapes=[pltpu.VMEM((2, SUBGRID + STRIP + 8, STRIP), f32), sem((2,))],
+            compiler_params=pltpu.CompilerParams(vmem_limit_bytes=8 * 1024 * 1024),
         )(column_place, grid)
         return grid.reshape(1, 1, 2, SUBGRID, STRIP)
 

time: 27.3 us -> 25.3 us (0.927)
  Pallas kernels: 26.5 us -> 24.4 us
    pallas_call x1, Pallas kernels: 24.7 us -> 23.6 us  [on_device(): pl.pallas_call(functools.partial(kernel, cols, facs), out_shape=jax.Shape...]
    pallas_call x1, Pallas kernels: 1.78 us -> 0.85 us  [on_device(): pl.pallas_call(place_kernel, out_shape=jax.ShapeDtypeStruct((2, SUBGRID,...]
where the time goes in v1:
time: 25.3 us; the launch traced here: 25.1 us
  Pallas kernels  24.4 us (96%)
  between operations  0.66 us (3%)
    pallas_call x1, Pallas kernels, on_device(): pl.pallas_call(functools.partial(kernel, cols, facs), out_shape=jax.Shape...  23.6 us
    pallas_call x1, Pallas kernels, on_device(): pl.pallas_call(place_kernel, out_shape=jax.ShapeDtypeStruct((2, SUBGRID,...  0.85 us

profile of v1, /device:TPU:0, one launch (start us, length us, event | category | flops | bytes accessed | tf_op | source)
XLA Modules:
  0.0 25.1 jit_solution(12027153303717363099)
XLA Ops:
  0.7 23.6 %shard_map.73.part = f32[2,128,128]{2,1,0:T(8,128)S(1)} custom-call(s32[4]{0:T(128)} %row_offset_in.1, s32[8]{0:T(128)} %column_offset_in.1, s32[4,8]{1,0:T(4,128)} %slot_subgrid_in.1, f32[1,1024]{1,0:T(1,128)} %bitcast.4, f32[1,4096]{1,0:T(1,128)} %bitcast.3, bf16[2,1024,512]{2,1,0:T(8,128)(2,1)} %facets.1), custom_call_target="tpu_custom_call" | custom-call | tf_op jit(solution)/shard_map/pallas_call | solution.py:283
  24.3 0.9 %shard_map.74 = f32[2,512,128]{2,1,0:T(8,128)} custom-call(s32[1]{0:T(128)S(6)} %copy.8.place, f32[2,128,128]{2,1,0:T(8,128)S(1)} %shard_map.73.part), custom_call_target="tpu_custom_call" | custom-call | tf_op jit(solution)/shard_map/pallas_call | solution.py:316

commit v2 on v1

v2 whole, which is shorter than its diff:
```python
import functools
import math

import jax
import jax.numpy as jnp
from jax import lax
from jax.experimental import pallas as pl
from jax.experimental.pallas import tpu as pltpu
from jax.sharding import PartitionSpec as P

FACET = 4096
STRIP = 128
SUBGRID = 512
FINE = 16
SIZES = (16, 16, 16, 16, 16, 16, 16, 16)
CHUNKS = len(SIZES)
HOP_ROWS = 68
HALVES = 2
HALF = STRIP // HALVES
MESH = pl.DeviceIdType.MESH


def unit_phase(phases):
    quarter = FACET // 4
    shifted = phases + quarter // 2
    angle = ((shifted & (quarter - 1)) - quarter // 2).astype(jnp.float32) * (2.0 * math.pi / FACET)
    turn = lax.shift_right_logical(shifted & (FACET - 1), quarter.bit_length() - 1)
    sq = angle * angle
    cosine = 1.0 + sq * (-1 / 2 + sq * (1 / 24 + sq * (-1 / 720 + sq * (1 / 40320))))
    sine = angle * (1.0 + sq * (-1 / 6 + sq * (1 / 120 + sq * (-1 / 5040 + sq * (1 / 362880)))))
    odd = (turn & 1) == 1
    first = jnp.where(odd, sine, cosine)
    second = jnp.where(odd, cosine, sine)
    real = jnp.where(((turn + 1) & 2) == 2, -first, first)
    imag = jnp.where((turn & 2) == 2, second, -second)
    return real, imag


def span(j):
    start = 2 * sum(SIZES[:j])
    return slice(start, start + 2 * SIZES[j])


def order():
    far_done, free, events = 0, 0, []
    for j, size in enumerate(SIZES):
        far_done += size
        free = max(free, far_done) + size
        events += [(far_done, 0, j), (free + HOP_ROWS, 1, j)]
    return [event[1:] for event in sorted(events)]


def chunks_of(half):
    return [j for j in range(CHUNKS) if sum(SIZES[:j]) // HALF == half]


def iota(shape, dim):
    return lax.broadcasted_iota(jnp.int32, shape, dim)


def kernel(
    cols, facs,
    row_offset_in, column_offset_in, slot_subgrid_in, row_taper_in, column_taper_in, facets,
    out,
    row_offset, column_offset, slot_subgrid, row_taper, column_gain, held, coarse_r, coarse_i, fine_r, fine_i, steep_r, steep_i, encode, decode_r, decode_i,
    pair_out, pair_in, far_part, far_out, far_in, own_part, strip, strip_in,
    partial, mine, sums, slots_out, slots_in,
    small_sem, held_sem, pair_send, pair_recv, far_send, far_recv, strip_send, strip_recv, slot_send, slot_recv,
):
    col = lax.axis_index("col")
    fac = lax.axis_index("fac")
    col_hi, core = col // 2, col % 2
    fac_hi, fac_lo = fac // 2, fac % 2
    highs, zs = cols // 2, facs // 2
    rows, width = facets.shape[1], facets.shape[2]

    pair_id = (col_hi * 2 + 1 - core, fac)
    far_ids = [((col_hi + d) % highs * 2 + core, fac) for d in range(1, highs)]
    strip_id = (col, fac_hi * 2 + 1 - fac_lo)
    slot_ids = [(col, (fac_hi + d) % zs * 2 + fac_lo) for d in range(1, zs)]
    peers = [pair_id, *far_ids, strip_id, *slot_ids]
    own_columns = pl.ds(pl.multiple_of(fac * width, width), width)
    small = [
        pltpu.make_async_copy(source, target, small_sem.at[n])
        for n, (source, target) in enumerate((
            (row_offset_in, row_offset), (column_offset_in, column_offset), (slot_subgrid_in, slot_subgrid),
            (row_taper_in, row_taper),
            (column_taper_in.at[:, own_columns], column_gain)))]
    loads = [pltpu.make_async_copy(facets.at[p], held.at[p], held_sem.at[p]) for p in range(2)]
    for load in (*small, *loads):
        load.start()
    barrier = pltpu.get_barrier_semaphore()
    for peer in peers:
        pl.semaphore_signal(barrier, inc=1, device_id=peer, device_id_type=MESH)

    steps = STRIP // FINE
    position = col * rows + iota((1, rows), 1)
    fine_r[...], fine_i[...] = unit_phase(iota((FINE, rows), 0) * position)
    for load in small:
        load.wait()
    gain = row_taper[...] * (1.0 / math.sqrt(FACET))

    def coarse(own, group):
        first = (row_offset[group] + FINE * iota((steps, rows), 0)) & (FACET - 1)
        real, imag = unit_phase(first * position)
        coarse_r[own] = real * gain
        coarse_i[own] = imag * gain

    def encode_half(index, own, half):
        def row(i, carry):
            source = pl.ds(half * (steps // HALVES) + i, 1)
            ar, ai = coarse_r[own, source, :], coarse_i[own, source, :]
            br, bi = fine_r[...], fine_i[...]
            at = pl.multiple_of(i * FINE, FINE) + half * 2 * HALF
            encode[index, pl.ds(at, FINE), :] = (ar * br - ai * bi).astype(jnp.bfloat16)
            encode[index, pl.ds(at + HALF, FINE), :] = (ar * bi + ai * br).astype(jnp.bfloat16)
            return carry

        lax.fori_loop(0, steps // HALVES, row, 0)

    def product(target, index, halves):
        table = encode[index, halves[0] * 2 * HALF:(halves[-1] + 1) * 2 * HALF]
        by_real, by_imag = [jnp.dot(table, held[p], preferred_element_type=jnp.float32) for p in range(2)]
        for n, half in enumerate(halves):
            at = n * 2 * HALF
            real = by_real[at:at + HALF] - by_imag[at + HALF:at + 2 * HALF]
            imag = by_imag[at:at + HALF] + by_real[at + HALF:at + 2 * HALF]
            for j in chunks_of(half):
                begin, size = span(j).start, SIZES[j]
                first = begin // 2 - half * HALF
                target[begin:begin + size] = real[first:first + size].astype(target.dtype)
                target[begin + size:begin + 2 * size] = imag[first:first + size].astype(target.dtype)

    def sends(source, target, send, recv, peer):
        return pltpu.make_async_remote_copy(
            src_ref=source, dst_ref=target, send_sem=send, recv_sem=recv, device_id=peer, device_id_type=MESH)

    def pair_copy(d, half):
        at = pl.ds(half * 2 * HALF, 2 * HALF)
        return sends(pair_out.at[d, at], pair_in.at[d, at], pair_send.at[0], pair_recv.at[d, half], pair_id)

    def far_copy(d, j):
        return sends(
            far_out.at[d - 1, span(j)], far_in.at[d - 1, span(j)], far_send.at[0], far_recv.at[d - 1, j], far_ids[d - 1])

    def strip_copy(j):
        return sends(strip.at[span(j)], strip_in.at[span(j)], strip_send.at[0], strip_recv.at[j], strip_id)

    def slot_copy(d, j):
        return sends(
            slots_out.at[d - 1, span(j)], slots_in.at[d - 1, span(j)], slot_send.at[0], slot_recv.at[j], slot_ids[d - 1])

    def slots_at(j):
        return sends(slots_out.at[:, span(j)], slots_in.at[:, span(j)], slot_send.at[0], slot_recv.at[j], strip_id)

    whole = range(HALVES)

    def group_of(d, own):
        return (col_hi + d) % highs * 2 + (core if own else 1 - core)

    def relay(d, half):
        pair_copy(d, half).wait_recv()
        for j in chunks_of(half):
            far_out[d - 1, span(j)] = (
                far_part[d - 1, span(j)] + pair_in[d, span(j)].astype(jnp.float32)).astype(jnp.bfloat16)
            far_copy(d, j).start()

    def send_pair(d, halves):
        for half in halves:
            pair_copy(d, half).start()

    for d in range(1, highs):
        for own in range(2):
            coarse(own, group_of(d, own))
            encode_half(2 * d + own, own, 0)
        if d == 1:
            for load in loads:
                load.wait()
        product(pair_out.at[d], 2 * d, [0])
        if d == 1:
            pl.semaphore_wait(barrier, len(peers))
        send_pair(d, [0])
        product(far_part.at[d - 1], 2 * d + 1, [0])
        for own in range(2):
            for half in whole[1:]:
                encode_half(2 * d + own, own, half)
        for half in whole[1:]:
            product(pair_out.at[d], 2 * d, [half])
            send_pair(d, [half])
        relay(d, 0)
        for half in whole[1:]:
            product(far_part.at[d - 1], 2 * d + 1, [half])
    for own in range(2):
        coarse(own, group_of(0, own))
        for half in whole:
            encode_half(own, own, half)
        if own == 0:
            product(pair_out.at[0], 0, whole)
            send_pair(0, whole)
            for d in range(1, highs):
                for half in whole[1:]:
                    relay(d, half)
    product(own_part, 1, whole)

    def decoded(block, part):
        at = slice(part * width, (part + 1) * width)
        size = block.shape[0] // 2
        by_real = jnp.dot(block, decode_r[at], preferred_element_type=jnp.float32)
        by_imag = jnp.dot(block, decode_i[at], preferred_element_type=jnp.float32)
        return jnp.concatenate([by_real[:size] - by_imag[size:], by_imag[:size] + by_real[size:]], axis=0)

    def arrive(j):
        if j in [chunks_of(half)[0] for half in whole]:
            pair_copy(0, span(j).start // (2 * HALF)).wait_recv()
        total = own_part[span(j)] + pair_in[0, span(j)].astype(jnp.float32)
        for d in range(1, highs):
            far_copy(d, j).wait_recv()
            total = total + far_in[d - 1, span(j)].astype(jnp.float32)
        strip[span(j)] = (total * column_gain[...]).astype(jnp.bfloat16)
        strip_copy(j).start()

    def finish(j):
        strip_copy(j).wait_recv()
        total = partial[span(j)] + decoded(strip_in[span(j)], 1)
        mine[span(j)] = total[:, :STRIP]
        for d in range(1, zs):
            slots_out[d - 1, span(j)] = total[:, d * STRIP:(d + 1) * STRIP].astype(jnp.bfloat16)
            slot_copy(d, j).start()

    lanes = zs * STRIP
    coarse_n = width // FINE
    starts = []
    for d in range(zs):
        start = column_offset[slot_subgrid[col, (fac_hi + d) % zs * 2 + fac_lo]]
        starts.append((start + iota((1, STRIP), 1)) & (FACET - 1))
    frequency = jnp.concatenate(starts, axis=1)
    fine_real, fine_imag = unit_phase(iota((FINE, lanes), 0) * frequency)
    fine_real, fine_imag = fine_real * (1.0 / math.sqrt(FACET)), fine_imag * (1.0 / math.sqrt(FACET))
    for part, block in enumerate((fac, fac_hi * 2 + 1 - fac_lo)):
        base = part * width
        steep_r[...], steep_i[...] = unit_phase((block * width + FINE * iota((coarse_n, lanes), 0)) * frequency)

        def row(i, carry, base=base):
            ar, ai = steep_r[pl.ds(i, 1), :], steep_i[pl.ds(i, 1), :]
            at = pl.multiple_of(base + i * FINE, FINE)
            decode_r[pl.ds(at, FINE), :] = (ar * fine_real - ai * fine_imag).astype(jnp.bfloat16)
            decode_i[pl.ds(at, FINE), :] = (ar * fine_imag + ai * fine_real).astype(jnp.bfloat16)
            return carry

        lax.fori_loop(0, coarse_n, row, 0)

    for stage, j in order():
        if stage == 0:
            arrive(j)
            partial[span(j)] = decoded(strip[span(j)], 0)
        else:
            finish(j)

    sends(pair_out, pair_in, pair_send.at[0], pair_recv.at[0, 0], pair_id).wait_send()
    if highs > 1:
        sends(far_out, far_in, far_send.at[0], far_recv.at[0, 0], far_ids[0]).wait_send()
    sends(strip, strip_in, strip_send.at[0], strip_recv.at[0], strip_id).wait_send()
    for j, size in enumerate(SIZES):
        total = mine[span(j)]
        slots_at(j).wait_recv()
        for d in range(1, zs):
            total = total + slots_in[d - 1, span(j)].astype(jnp.float32)
        first = span(j).start // 2
        for p in range(2):
            sums[p, first:first + size] = total[p * size:(p + 1) * size]
    for p in range(2):
        out[p] = sums[p].T
    sends(slots_out, slots_in, slot_send.at[0], slot_recv.at[0], strip_id).wait_send()


def place_kernel(place, part, out, grid, sem):
    shift = lax.rem(place[0], 8)
    first = pl.multiple_of(place[0] - shift, 8)
    band = STRIP + 8
    copies = [pltpu.make_async_copy(grid.at[n, pl.ds(0, SUBGRID)], out.at[n], sem.at[n]) for n in range(2)]
    for n in range(2):
        grid[n] = jnp.zeros(grid.shape[1:], jnp.float32)
        grid[n, pl.ds(first, band)] = pltpu.roll(
            jnp.concatenate([part[n], jnp.zeros((8, STRIP), jnp.float32)], axis=0), shift, 0)
        grid[n, :band] += grid[n, SUBGRID:]
        copies[n].start()
    for copy in copies:
        copy.wait()


def solution(mesh):
    cols, facs = mesh.shape["col"], mesh.shape["fac"]
    highs, zs = cols // 2, facs // 2

    def on_device(facets, row_taper, column_taper, column_place, row_offset, column_offset, slot_subgrid):
        rows, width = facets.shape[1], facets.shape[2]
        bf16, f32 = jnp.bfloat16, jnp.float32
        lanes = zs * STRIP
        part = (2 * STRIP, width)
        slot = (2 * STRIP, STRIP)
        far = max(highs - 1, 1)
        sem = pltpu.SemaphoreType.DMA
        grid = pl.pallas_call(
            functools.partial(kernel, cols, facs),
            out_shape=jax.ShapeDtypeStruct((2, STRIP, STRIP), f32),
            in_specs=[pl.BlockSpec(memory_space=pltpu.HBM)] * 6,
            out_specs=pl.BlockSpec(memory_space=pltpu.VMEM),
            scratch_shapes=[
                pltpu.SMEM(row_offset.shape, jnp.int32), pltpu.SMEM(column_offset.shape, jnp.int32),
                pltpu.SMEM(slot_subgrid.shape, jnp.int32),
                pltpu.VMEM((1, rows), f32), pltpu.VMEM((1, width), f32),
                pltpu.VMEM((2, rows, width), bf16),
                pltpu.VMEM((2, STRIP // FINE, rows), f32), pltpu.VMEM((2, STRIP // FINE, rows), f32),
                pltpu.VMEM((FINE, rows), f32), pltpu.VMEM((FINE, rows), f32),
                pltpu.VMEM((width // FINE, lanes), f32), pltpu.VMEM((width // FINE, lanes), f32),
                pltpu.VMEM((cols, 2 * STRIP, rows), bf16),
                pltpu.VMEM((2 * width, lanes), bf16), pltpu.VMEM((2 * width, lanes), bf16),
                pltpu.VMEM((highs, *part), bf16), pltpu.VMEM((highs, *part), bf16),
                pltpu.VMEM((far, *part), f32),
                pltpu.VMEM((far, *part), bf16), pltpu.VMEM((far, *part), bf16),
                pltpu.VMEM(part, f32),
                pltpu.VMEM(part, bf16), pltpu.VMEM(part, bf16),
                pltpu.VMEM((2 * STRIP, lanes), f32),
                pltpu.VMEM(slot, f32), pltpu.VMEM((2, STRIP, STRIP), f32),
                pltpu.VMEM((zs - 1, *slot), bf16), pltpu.VMEM((zs - 1, *slot), bf16),
                sem((5,)), sem((2,)),
                sem((1,)), sem((highs, HALVES)),
                sem((1,)), sem((far, CHUNKS)),
                sem((1,)), sem((CHUNKS,)),
                sem((1,)), sem((CHUNKS,)),
            ],
            compiler_params=pltpu.CompilerParams(
                collective_id=0, has_side_effects=True, vmem_limit_bytes=32 * 1024 * 1024),
        )(*[pltpu.with_memory_space_constraint(value, pltpu.HBM) for value in (
            row_offset, column_offset, slot_subgrid, row_taper.reshape(1, -1), column_taper.reshape(1, -1), facets)])
        grid = pl.pallas_call(
            place_kernel,
            out_shape=jax.ShapeDtypeStruct((2, SUBGRID, STRIP), f32),
            in_specs=[pl.BlockSpec(memory_space=pltpu.SMEM), pl.BlockSpec(memory_space=pltpu.VMEM)],
            out_specs=pl.BlockSpec(memory_space=pltpu.HBM),
            scratch_shapes=[pltpu.VMEM((2, SUBGRID + STRIP + 8, STRIP), f32), sem((2,))],
            compiler_params=pltpu.CompilerParams(vmem_limit_bytes=8 * 1024 * 1024),
        )(column_place, grid)
        return grid.reshape(1, 1, 2, SUBGRID, STRIP)

    in_specs = (P(None, "col", "fac"), P("col"), P(), P(), P(), P(), P())
    out_specs = P("col", "fac", None, None, None)
    return jax.shard_map(on_device, mesh=mesh, in_specs=in_specs, out_specs=out_specs, check_vma=False)
```

time: 25.3 us -> 24.2 us (0.957)
  Pallas kernels: 24.4 us -> 23.4 us
    pallas_call x1, Pallas kernels: 23.6 us -> 22.5 us  [on_device(): pl.pallas_call(functools.partial(kernel, cols, facs), out_shape=jax.Shape...]
where the time goes in v2:
time: 24.2 us; the launch traced here: 24 us
  Pallas kernels  23.4 us (97%)
  between operations  0.66 us (3%)
    pallas_call x1, Pallas kernels, on_device(): pl.pallas_call(functools.partial(kernel, cols, facs), out_shape=jax.Shape...  22.5 us
    pallas_call x1, Pallas kernels, on_device(): pl.pallas_call(place_kernel, out_shape=jax.ShapeDtypeStruct((2, SUBGRID,...  0.85 us

profile of v2, /device:TPU:0, one launch (start us, length us, event | category | flops | bytes accessed | tf_op | source)
XLA Modules:
  0.0 24.0 jit_solution(14537620107565767748)
XLA Ops:
  0.7 22.5 %shard_map.73.part = f32[2,128,128]{2,1,0:T(8,128)S(1)} custom-call(s32[4]{0:T(128)} %row_offset_in.1, s32[8]{0:T(128)} %column_offset_in.1, s32[4,8]{1,0:T(4,128)} %slot_subgrid_in.1, f32[1,1024]{1,0:T(1,128)} %bitcast.4, f32[1,4096]{1,0:T(1,128)} %bitcast.3, bf16[2,1024,512]{2,1,0:T(8,128)(2,1)} %facets.1), custom_call_target="tpu_custom_call" | custom-call | tf_op jit(solution)/shard_map/pallas_call | solution.py:303
  23.2 0.9 %shard_map.74 = f32[2,512,128]{2,1,0:T(8,128)} custom-call(s32[1]{0:T(128)S(6)} %copy.8.place, f32[2,128,128]{2,1,0:T(8,128)S(1)} %shard_map.73.part), custom_call_target="tpu_custom_call" | custom-call | tf_op jit(solution)/shard_map/pallas_call | solution.py:336

commit v3 on v2

--- a/solution.py
+++ b/solution.py
@@ -148,10 +148,12 @@
 
     def slot_copy(d, j):
         return sends(
-            slots_out.at[d - 1, span(j)], slots_in.at[d - 1, span(j)], slot_send.at[0], slot_recv.at[j], slot_ids[d - 1])
-
-    def slots_at(j):
-        return sends(slots_out.at[:, span(j)], slots_in.at[:, span(j)], slot_send.at[0], slot_recv.at[j], strip_id)
+            slots_out.at[d - 1, span(j)], slots_in.at[d - 1, span(j)], slot_send.at[0], slot_recv.at[j // (CHUNKS - 1)], slot_ids[d - 1])
+
+    def slots_wait(last):
+        edge = span(CHUNKS - 1).start
+        at = slice(edge, 2 * STRIP) if last else slice(0, edge)
+        sends(slots_out.at[:, at], slots_in.at[:, at], slot_send.at[0], slot_recv.at[last], strip_id).wait_recv()
 
     whole = range(HALVES)
 
@@ -170,9 +172,8 @@
             pair_copy(d, half).start()
 
     for d in range(1, highs):
-        for own in range(2):
-            coarse(own, group_of(d, own))
-            encode_half(2 * d + own, own, 0)
+        coarse(0, group_of(d, 0))
+        encode_half(2 * d, 0, 0)
         if d == 1:
             for load in loads:
                 load.wait()
@@ -180,14 +181,16 @@
         if d == 1:
             pl.semaphore_wait(barrier, len(peers))
         send_pair(d, [0])
+        coarse(1, group_of(d, 1))
+        encode_half(2 * d + 1, 1, 0)
         product(far_part.at[d - 1], 2 * d + 1, [0])
         for own in range(2):
             for half in whole[1:]:
                 encode_half(2 * d + own, own, half)
+        relay(d, 0)
         for half in whole[1:]:
             product(pair_out.at[d], 2 * d, [half])
             send_pair(d, [half])
-        relay(d, 0)
         for half in whole[1:]:
             product(far_part.at[d - 1], 2 * d + 1, [half])
     for own in range(2):
@@ -202,12 +205,11 @@
                     relay(d, half)
     product(own_part, 1, whole)
 
-    def decoded(block, part):
-        at = slice(part * width, (part + 1) * width)
+    def decoded(block):
         size = block.shape[0] // 2
-        by_real = jnp.dot(block, decode_r[at], preferred_element_type=jnp.float32)
-        by_imag = jnp.dot(block, decode_i[at], preferred_element_type=jnp.float32)
-        return jnp.concatenate([by_real[:size] - by_imag[size:], by_imag[:size] + by_real[size:]], axis=0)
+        by_real = jnp.dot(block, decode_r[...], preferred_element_type=jnp.float32)
+        by_imag = jnp.dot(block, decode_i[...], preferred_element_type=jnp.float32)
+        return by_real[:size] - by_imag[size:], by_imag[:size] + by_real[size:]
 
     def arrive(j):
         if j in [chunks_of(half)[0] for half in whole]:
@@ -221,7 +223,9 @@
 
     def finish(j):
         strip_copy(j).wait_recv()
-        total = partial[span(j)] + decoded(strip_in[span(j)], 1)
+        real, imag = decoded(strip_in[span(j)])
+        total = partial[span(j)] + jnp.concatenate(
+            [real * shift_real - imag * shift_imag, imag * shift_real + real * shift_imag], axis=0)
         mine[span(j)] = total[:, :STRIP]
         for d in range(1, zs):
             slots_out[d - 1, span(j)] = total[:, d * STRIP:(d + 1) * STRIP].astype(jnp.bfloat16)
@@ -236,23 +240,22 @@
     frequency = jnp.concatenate(starts, axis=1)
     fine_real, fine_imag = unit_phase(iota((FINE, lanes), 0) * frequency)
     fine_real, fine_imag = fine_real * (1.0 / math.sqrt(FACET)), fine_imag * (1.0 / math.sqrt(FACET))
-    for part, block in enumerate((fac, fac_hi * 2 + 1 - fac_lo)):
-        base = part * width
-        steep_r[...], steep_i[...] = unit_phase((block * width + FINE * iota((coarse_n, lanes), 0)) * frequency)
-
-        def row(i, carry, base=base):
-            ar, ai = steep_r[pl.ds(i, 1), :], steep_i[pl.ds(i, 1), :]
-            at = pl.multiple_of(base + i * FINE, FINE)
-            decode_r[pl.ds(at, FINE), :] = (ar * fine_real - ai * fine_imag).astype(jnp.bfloat16)
-            decode_i[pl.ds(at, FINE), :] = (ar * fine_imag + ai * fine_real).astype(jnp.bfloat16)
-            return carry
-
-        lax.fori_loop(0, coarse_n, row, 0)
+    steep_r[...], steep_i[...] = unit_phase((fac * width + FINE * iota((coarse_n, lanes), 0)) * frequency)
+    shift_real, shift_imag = unit_phase((1 - 2 * fac_lo) * width * frequency)
+
+    def row(i, carry):
+        ar, ai = steep_r[pl.ds(i, 1), :], steep_i[pl.ds(i, 1), :]
+        at = pl.multiple_of(i * FINE, FINE)
+        decode_r[pl.ds(at, FINE), :] = (ar * fine_real - ai * fine_imag).astype(jnp.bfloat16)
+        decode_i[pl.ds(at, FINE), :] = (ar * fine_imag + ai * fine_real).astype(jnp.bfloat16)
+        return carry
+
+    lax.fori_loop(0, coarse_n, row, 0)
 
     for stage, j in order():
         if stage == 0:
             arrive(j)
-            partial[span(j)] = decoded(strip[span(j)], 0)
+            partial[span(j)] = jnp.concatenate(decoded(strip[span(j)]), axis=0)
         else:
             finish(j)
 
@@ -262,7 +265,8 @@
     sends(strip, strip_in, strip_send.at[0], strip_recv.at[0], strip_id).wait_send()
     for j, size in enumerate(SIZES):
         total = mine[span(j)]
-        slots_at(j).wait_recv()
+        if j in (0, CHUNKS - 1):
+            slots_wait(j // (CHUNKS - 1))
         for d in range(1, zs):
             total = total + slots_in[d - 1, span(j)].astype(jnp.float32)
         first = span(j).start // 2
@@ -314,7 +318,7 @@
                 pltpu.VMEM((FINE, rows), f32), pltpu.VMEM((FINE, rows), f32),
                 pltpu.VMEM((width // FINE, lanes), f32), pltpu.VMEM((width // FINE, lanes), f32),
                 pltpu.VMEM((cols, 2 * STRIP, rows), bf16),
-                pltpu.VMEM((2 * width, lanes), bf16), pltpu.VMEM((2 * width, lanes), bf16),
+                pltpu.VMEM((width, lanes), bf16), pltpu.VMEM((width, lanes), bf16),
                 pltpu.VMEM((highs, *part), bf16), pltpu.VMEM((highs, *part), bf16),
                 pltpu.VMEM((far, *part), f32),
                 pltpu.VMEM((far, *part), bf16), pltpu.VMEM((far, *part), bf16),
@@ -327,7 +331,7 @@
                 sem((1,)), sem((highs, HALVES)),
                 sem((1,)), sem((far, CHUNKS)),
                 sem((1,)), sem((CHUNKS,)),
-                sem((1,)), sem((CHUNKS,)),
+                sem((1,)), sem((2,)),
             ],
             compiler_params=pltpu.CompilerParams(
                 collective_id=0, has_side_effects=True, vmem_limit_bytes=32 * 1024 * 1024),

time: 24.2 us -> 23.9 us (0.988)
  Pallas kernels: 23.4 us -> 23.1 us
    pallas_call x1, Pallas kernels: 22.5 us -> 22.2 us  [on_device(): pl.pallas_call(functools.partial(kernel, cols, facs), out_shape=jax.Shape...]
where the time goes in v3:
time: 23.9 us; the launch traced here: 23.7 us
  Pallas kernels  23.1 us (97%)
  between operations  0.66 us (3%)
    pallas_call x1, Pallas kernels, on_device(): pl.pallas_call(functools.partial(kernel, cols, facs), out_shape=jax.Shape...  22.2 us
    pallas_call x1, Pallas kernels, on_device(): pl.pallas_call(place_kernel, out_shape=jax.ShapeDtypeStruct((2, SUBGRID,...  0.85 us

profile of v3, /device:TPU:0, one launch (start us, length us, event | category | flops | bytes accessed | tf_op | source)
XLA Modules:
  0.0 23.7 jit_solution(1664517963620179367)
XLA Ops:
  0.7 22.2 %shard_map.73.part = f32[2,128,128]{2,1,0:T(8,128)S(1)} custom-call(s32[4]{0:T(128)} %row_offset_in.1, s32[8]{0:T(128)} %column_offset_in.1, s32[4,8]{1,0:T(4,128)} %slot_subgrid_in.1, f32[1,1024]{1,0:T(1,128)} %bitcast.4, f32[1,4096]{1,0:T(1,128)} %bitcast.3, bf16[2,1024,512]{2,1,0:T(8,128)(2,1)} %facets.1), custom_call_target="tpu_custom_call" | custom-call | tf_op jit(solution)/shard_map/pallas_call | solution.py:307
  22.9 0.9 %shard_map.74 = f32[2,512,128]{2,1,0:T(8,128)} custom-call(s32[1]{0:T(128)S(6)} %copy.8.place, f32[2,128,128]{2,1,0:T(8,128)S(1)} %shard_map.73.part), custom_call_target="tpu_custom_call" | custom-call | tf_op jit(solution)/shard_map/pallas_call | solution.py:340

commit v4 on v3

--- a/solution.py
+++ b/solution.py
@@ -15,6 +15,7 @@
 SIZES = (16, 16, 16, 16, 16, 16, 16, 16)
 CHUNKS = len(SIZES)
 HOP_ROWS = 68
+LEAD = 2
 HALVES = 2
 HALF = STRIP // HALVES
 MESH = pl.DeviceIdType.MESH
@@ -171,38 +172,71 @@
         for half in halves:
             pair_copy(d, half).start()
 
-    for d in range(1, highs):
-        coarse(0, group_of(d, 0))
-        encode_half(2 * d, 0, 0)
+    def near(d, half):
+        product(pair_out.at[d], 2 * d, [half])
+        send_pair(d, [half])
+
+    def far(d, half):
+        product(far_part.at[d - 1], 2 * d + 1, [half])
+
+    def table(d, own):
+        coarse(own, group_of(d, own))
+        encode_half(2 * d + own, own, 0)
+
+    def enter(d):
+        if d == 1:
+            pl.semaphore_wait(barrier, len(peers))
+
+    def ready(d):
         if d == 1:
             for load in loads:
                 load.wait()
-        product(pair_out.at[d], 2 * d, [0])
-        if d == 1:
-            pl.semaphore_wait(barrier, len(peers))
-        send_pair(d, [0])
-        coarse(1, group_of(d, 1))
-        encode_half(2 * d + 1, 1, 0)
-        product(far_part.at[d - 1], 2 * d + 1, [0])
-        for own in range(2):
-            for half in whole[1:]:
-                encode_half(2 * d + own, own, half)
-        relay(d, 0)
-        for half in whole[1:]:
-            product(pair_out.at[d], 2 * d, [half])
-            send_pair(d, [half])
-        for half in whole[1:]:
-            product(far_part.at[d - 1], 2 * d + 1, [half])
-    for own in range(2):
-        coarse(own, group_of(0, own))
-        for half in whole:
-            encode_half(own, own, half)
-        if own == 0:
-            product(pair_out.at[0], 0, whole)
-            send_pair(0, whole)
+
+    @pl.when(core == 0)
+    def _():
+        for d in range(1, highs):
+            table(d, 1)
+            ready(d)
+            far(d, 0)
+            enter(d)
+            table(d, 0)
+            relay(d, 0)
+            near(d, 0)
+            for own in range(2):
+                encode_half(2 * d + own, own, 1)
+            far(d, 1)
+            near(d, 1)
+            relay(d, 1)
+
+    @pl.when(core == 1)
+    def _():
+        for d in range(1, highs):
+            table(d, 0)
+            ready(d)
+            product(pair_out.at[d], 2 * d, [0])
+            enter(d)
+            send_pair(d, [0])
+            table(d, 1)
+            far(d, 0)
+            for own in range(2):
+                encode_half(2 * d + own, own, 1)
+            near(d, 1)
+            far(d, 1)
+
+    def relays(half):
+        @pl.when(core == 1)
+        def _():
             for d in range(1, highs):
-                for half in whole[1:]:
-                    relay(d, half)
+                relay(d, half)
+
+    table(0, 0)
+    encode_half(0, 0, 1)
+    relays(0)
+    product(pair_out.at[0], 0, whole)
+    send_pair(0, whole)
+    table(0, 1)
+    encode_half(1, 1, 1)
+    relays(1)
     product(own_part, 1, whole)
 
     def decoded(block):
@@ -225,37 +259,44 @@
         strip_copy(j).wait_recv()
         real, imag = decoded(strip_in[span(j)])
         total = partial[span(j)] + jnp.concatenate(
-            [real * shift_real - imag * shift_imag, imag * shift_real + real * shift_imag], axis=0)
+            [real * turn[0] - imag * turn[1], imag * turn[0] + real * turn[1]], axis=0)
         mine[span(j)] = total[:, :STRIP]
         for d in range(1, zs):
             slots_out[d - 1, span(j)] = total[:, d * STRIP:(d + 1) * STRIP].astype(jnp.bfloat16)
             slot_copy(d, j).start()
 
-    lanes = zs * STRIP
-    coarse_n = width // FINE
-    starts = []
-    for d in range(zs):
-        start = column_offset[slot_subgrid[col, (fac_hi + d) % zs * 2 + fac_lo]]
-        starts.append((start + iota((1, STRIP), 1)) & (FACET - 1))
-    frequency = jnp.concatenate(starts, axis=1)
-    fine_real, fine_imag = unit_phase(iota((FINE, lanes), 0) * frequency)
-    fine_real, fine_imag = fine_real * (1.0 / math.sqrt(FACET)), fine_imag * (1.0 / math.sqrt(FACET))
-    steep_r[...], steep_i[...] = unit_phase((fac * width + FINE * iota((coarse_n, lanes), 0)) * frequency)
-    shift_real, shift_imag = unit_phase((1 - 2 * fac_lo) * width * frequency)
-
-    def row(i, carry):
-        ar, ai = steep_r[pl.ds(i, 1), :], steep_i[pl.ds(i, 1), :]
-        at = pl.multiple_of(i * FINE, FINE)
-        decode_r[pl.ds(at, FINE), :] = (ar * fine_real - ai * fine_imag).astype(jnp.bfloat16)
-        decode_i[pl.ds(at, FINE), :] = (ar * fine_imag + ai * fine_real).astype(jnp.bfloat16)
-        return carry
-
-    lax.fori_loop(0, coarse_n, row, 0)
+    turn = []
+
+    def decode_tables():
+        lanes = zs * STRIP
+        coarse_n = width // FINE
+        starts = []
+        for d in range(zs):
+            start = column_offset[slot_subgrid[col, (fac_hi + d) % zs * 2 + fac_lo]]
+            starts.append((start + iota((1, STRIP), 1)) & (FACET - 1))
+        frequency = jnp.concatenate(starts, axis=1)
+        fine_real, fine_imag = unit_phase(iota((FINE, lanes), 0) * frequency)
+        fine_real, fine_imag = fine_real * (1.0 / math.sqrt(FACET)), fine_imag * (1.0 / math.sqrt(FACET))
+        steep_r[...], steep_i[...] = unit_phase((fac * width + FINE * iota((coarse_n, lanes), 0)) * frequency)
+        shift_real, shift_imag = unit_phase((1 - 2 * fac_lo) * width * frequency)
+
+        def row(i, carry):
+            ar, ai = steep_r[pl.ds(i, 1), :], steep_i[pl.ds(i, 1), :]
+            at = pl.multiple_of(i * FINE, FINE)
+            decode_r[pl.ds(at, FINE), :] = (ar * fine_real - ai * fine_imag).astype(jnp.bfloat16)
+            decode_i[pl.ds(at, FINE), :] = (ar * fine_imag + ai * fine_real).astype(jnp.bfloat16)
+            return carry
+
+        lax.fori_loop(0, coarse_n, row, 0)
+        turn.extend((shift_real, shift_imag))
 
     for stage, j in order():
         if stage == 0:
             arrive(j)
-            partial[span(j)] = jnp.concatenate(decoded(strip[span(j)]), axis=0)
+            if j == LEAD:
+                decode_tables()
+            for done in range(j + 1) if j == LEAD else [j] if j > LEAD else []:
+                partial[span(done)] = jnp.concatenate(decoded(strip[span(done)]), axis=0)
         else:
             finish(j)
 

time: 23.9 us -> 23.3 us (0.975)
  Pallas kernels: 23.1 us -> 22.3 us
    pallas_call x1, Pallas kernels: 22.2 us -> 21.4 us  [on_device(): pl.pallas_call(functools.partial(kernel, cols, facs), out_shape=jax.Shape...]
where the time goes in v4:
time: 23.3 us; the launch traced here: 23 us
  Pallas kernels  22.3 us (96%)
  between operations  0.66 us (3%)
    pallas_call x1, Pallas kernels, on_device(): pl.pallas_call(functools.partial(kernel, cols, facs), out_shape=jax.Shape...  21.4 us
    pallas_call x1, Pallas kernels, on_device(): pl.pallas_call(place_kernel, out_shape=jax.ShapeDtypeStruct((2, SUBGRID,...  0.85 us

profile of v4, /device:TPU:0, one launch (start us, length us, event | category | flops | bytes accessed | tf_op | source)
XLA Modules:
  0.0 23.0 jit_solution(9375195246210173433)
XLA Ops:
  0.7 21.4 %shard_map.73.part = f32[2,128,128]{2,1,0:T(8,128)S(1)} custom-call(s32[4]{0:T(128)} %row_offset_in.1, s32[8]{0:T(128)} %column_offset_in.1, s32[4,8]{1,0:T(4,128)} %slot_subgrid_in.1, f32[1,1024]{1,0:T(1,128)} %bitcast.4, f32[1,4096]{1,0:T(1,128)} %bitcast.3, bf16[2,1024,512]{2,1,0:T(8,128)(2,1)} %facets.1), custom_call_target="tpu_custom_call" | custom-call | tf_op jit(solution)/shard_map/pallas_call | solution.py:348
  22.1 0.9 %shard_map.74 = f32[2,512,128]{2,1,0:T(8,128)} custom-call(s32[1]{0:T(128)S(6)} %copy.8.place, f32[2,128,128]{2,1,0:T(8,128)S(1)} %shard_map.73.part), custom_call_target="tpu_custom_call" | custom-call | tf_op jit(solution)/shard_map/pallas_call | solution.py:381

commit v5 on v4

--- a/solution.py
+++ b/solution.py
@@ -87,7 +87,7 @@
             (row_offset_in, row_offset), (column_offset_in, column_offset), (slot_subgrid_in, slot_subgrid),
             (row_taper_in, row_taper),
             (column_taper_in.at[:, own_columns], column_gain)))]
-    loads = [pltpu.make_async_copy(facets.at[p], held.at[p], held_sem.at[p]) for p in range(2)]
+    loads = [pltpu.make_async_copy(facets.at[p, pl.ds(q * rows // 4, rows // 4)], held.at[p, pl.ds(q * rows // 4, rows // 4)], held_sem.at[4 * p + q]) for p in range(2) for q in range(4)]
     for load in (*small, *loads):
         load.start()
     barrier = pltpu.get_barrier_semaphore()
@@ -200,10 +200,13 @@
             far(d, 0)
             enter(d)
             table(d, 0)
+            for own in range(2):
+                encode_half(2 * d + own, own, 1)
+            if d == highs - 1:
+                table(0, 0)
+                encode_half(0, 0, 1)
             relay(d, 0)
             near(d, 0)
-            for own in range(2):
-                encode_half(2 * d + own, own, 1)
             far(d, 1)
             near(d, 1)
             relay(d, 1)
@@ -222,6 +225,8 @@
                 encode_half(2 * d + own, own, 1)
             near(d, 1)
             far(d, 1)
+        table(0, 0)
+        encode_half(0, 0, 1)
 
     def relays(half):
         @pl.when(core == 1)
@@ -229,11 +234,9 @@
             for d in range(1, highs):
                 relay(d, half)
 
-    table(0, 0)
-    encode_half(0, 0, 1)
-    relays(0)
     product(pair_out.at[0], 0, whole)
     send_pair(0, whole)
+    relays(0)
     table(0, 1)
     encode_half(1, 1, 1)
     relays(1)
@@ -368,7 +371,7 @@
                 pltpu.VMEM((2 * STRIP, lanes), f32),
                 pltpu.VMEM(slot, f32), pltpu.VMEM((2, STRIP, STRIP), f32),
                 pltpu.VMEM((zs - 1, *slot), bf16), pltpu.VMEM((zs - 1, *slot), bf16),
-                sem((5,)), sem((2,)),
+                sem((5,)), sem((8,)),
                 sem((1,)), sem((highs, HALVES)),
                 sem((1,)), sem((far, CHUNKS)),
                 sem((1,)), sem((CHUNKS,)),

time: 23.3 us -> 23.2 us (level)
  no operation moved by 1% of the time
where the time goes in v5:
time: 23.2 us; the launch traced here: 23 us
  Pallas kernels  22.3 us (96%)
  between operations  0.66 us (3%)
    pallas_call x1, Pallas kernels, on_device(): pl.pallas_call(functools.partial(kernel, cols, facs), out_shape=jax.Shape...  21.5 us
    pallas_call x1, Pallas kernels, on_device(): pl.pallas_call(place_kernel, out_shape=jax.ShapeDtypeStruct((2, SUBGRID,...  0.85 us

profile of v5, /device:TPU:0, one launch (start us, length us, event | category | flops | bytes accessed | tf_op | source)
XLA Modules:
  0.0 23.0 jit_solution(7093087194740618820)
XLA Ops:
  0.7 21.5 %shard_map.73.part = f32[2,128,128]{2,1,0:T(8,128)S(1)} custom-call(s32[4]{0:T(128)} %row_offset_in.1, s32[8]{0:T(128)} %column_offset_in.1, s32[4,8]{1,0:T(4,128)} %slot_subgrid_in.1, f32[1,1024]{1,0:T(1,128)} %bitcast.4, f32[1,4096]{1,0:T(1,128)} %bitcast.3, bf16[2,1024,512]{2,1,0:T(8,128)(2,1)} %facets.1), custom_call_target="tpu_custom_call" | custom-call | tf_op jit(solution)/shard_map/pallas_call | solution.py:351
  22.1 0.9 %shard_map.74 = f32[2,512,128]{2,1,0:T(8,128)} custom-call(s32[1]{0:T(128)S(6)} %copy.8.place, f32[2,128,128]{2,1,0:T(8,128)S(1)} %shard_map.73.part), custom_call_target="tpu_custom_call" | custom-call | tf_op jit(solution)/shard_map/pallas_call | solution.py:384

commit v6 on v5

--- a/solution.py
+++ b/solution.py
@@ -14,7 +14,7 @@
 FINE = 16
 SIZES = (16, 16, 16, 16, 16, 16, 16, 16)
 CHUNKS = len(SIZES)
-HOP_ROWS = 68
+HOP_ROWS = 48
 LEAD = 2
 HALVES = 2
 HALF = STRIP // HALVES
@@ -87,7 +87,7 @@
             (row_offset_in, row_offset), (column_offset_in, column_offset), (slot_subgrid_in, slot_subgrid),
             (row_taper_in, row_taper),
             (column_taper_in.at[:, own_columns], column_gain)))]
-    loads = [pltpu.make_async_copy(facets.at[p, pl.ds(q * rows // 4, rows // 4)], held.at[p, pl.ds(q * rows // 4, rows // 4)], held_sem.at[4 * p + q]) for p in range(2) for q in range(4)]
+    loads = [pltpu.make_async_copy(facets.at[p], held.at[p], held_sem.at[p]) for p in range(2)]
     for load in (*small, *loads):
         load.start()
     barrier = pltpu.get_barrier_semaphore()
@@ -371,7 +371,7 @@
                 pltpu.VMEM((2 * STRIP, lanes), f32),
                 pltpu.VMEM(slot, f32), pltpu.VMEM((2, STRIP, STRIP), f32),
                 pltpu.VMEM((zs - 1, *slot), bf16), pltpu.VMEM((zs - 1, *slot), bf16),
-                sem((5,)), sem((8,)),
+                sem((5,)), sem((2,)),
                 sem((1,)), sem((highs, HALVES)),
                 sem((1,)), sem((far, CHUNKS)),
                 sem((1,)), sem((CHUNKS,)),

time: 23.2 us -> 23.2 us (level)
  no operation moved by 1% of the time
where the time goes in v6:
time: 23.2 us; the launch traced here: 23 us
  Pallas kernels  22.4 us (97%)
  between operations  0.66 us (3%)
    pallas_call x1, Pallas kernels, on_device(): pl.pallas_call(functools.partial(kernel, cols, facs), out_shape=jax.Shape...  21.5 us
    pallas_call x1, Pallas kernels, on_device(): pl.pallas_call(place_kernel, out_shape=jax.ShapeDtypeStruct((2, SUBGRID,...  0.85 us

profile of v6, /device:TPU:0, one launch (start us, length us, event | category | flops | bytes accessed | tf_op | source)
XLA Modules:
  0.0 23.0 jit_solution(3145653133061013967)
XLA Ops:
  0.7 21.5 %shard_map.73.part = f32[2,128,128]{2,1,0:T(8,128)S(1)} custom-call(s32[4]{0:T(128)} %row_offset_in.1, s32[8]{0:T(128)} %column_offset_in.1, s32[4,8]{1,0:T(4,128)} %slot_subgrid_in.1, f32[1,1024]{1,0:T(1,128)} %bitcast.4, f32[1,4096]{1,0:T(1,128)} %bitcast.3, bf16[2,1024,512]{2,1,0:T(8,128)(2,1)} %facets.1), custom_call_target="tpu_custom_call" | custom-call | tf_op jit(solution)/shard_map/pallas_call | solution.py:351
  22.2 0.9 %shard_map.74 = f32[2,512,128]{2,1,0:T(8,128)} custom-call(s32[1]{0:T(128)S(6)} %copy.8.place, f32[2,128,128]{2,1,0:T(8,128)S(1)} %shard_map.73.part), custom_call_target="tpu_custom_call" | custom-call | tf_op jit(solution)/shard_map/pallas_call | solution.py:384
